TPU v7x, 32 devices: a whole 2x2x4 slice. The times are simulated.
32 devices in a mesh: dom: 32 (over z, y, x, core).
Axes of the slice: x: 2, y: 2, z: 4, core: 2. Of those that a mesh axis runs over, the one named last changes fastest.
Arguments:
- rest_pos: float32 [3, 131072], P(None, 'dom'), may hold values from -6 to 6
- displacement: float32 [3, 131072], P(None, 'dom'), may hold values from -3 to 3
- velocity: float32 [3, 131072], P(None, 'dom'), may hold values from -6 to 6
- ext_force: float32 [3, 131072], P(None, 'dom'), may hold values from -6 to 6
- node_mass: float32 [131072], P('dom'), may hold values from 0.5 to 2
- body_accel: float32 [3], replicated, may hold values from -2 to 2
- connectivity: int32 [8, 131072], P(None, 'dom'), may hold values from 0 to 4095
- elem_material: int32 [1024], P('dom'), may hold values from 0 to 7
- stiffness: float32 [8, 24, 24], replicated, may hold values from -1.25 to 1.25
- shared_nodes: int32 [32, 5, 128], P('dom'), may hold values from 0 to 4095, as said below
- contact_slave: int32 [65536], P('dom'), may hold values from 0 to 4095
- contact_owner: int32 [65536, 1], P('dom'), may hold values from 0 to 31; in each aligned block of 2048 rows (0 to 2047, 2048 to 4095, ...) at most 256 rows name the same one
- contact_master: int32 [65536], P('dom'), may hold values from 0 to 4095
- contact_normal: float32 [3, 65536], P(None, 'dom'), may hold values from -4 to 4
- part_of_node: int32 [131072], P('dom'), may hold values from 0 to 799
- part_mass: float32 [400], replicated, may hold values from 81 to 327
- part_center: float32 [3, 400], replicated, may hold values from -1 to 1
- part_inertia: float32 [3, 400], replicated, may hold values from 81 to 327
Outputs:
- nodal_velocity: float32 [3, 131072], P(None, 'dom')
- part_motion: float32 [6, 400], replicated
Inputs may be any that keep to these rules, and one draw needn't show every extreme that they name: `connectivity`: offsets are taken modulo 4096 after adding the element's own local number. `shared_nodes`: on each partition d the 5 x 128 entries are distinct interface copies; entry k of list b on d and entry k of list b on d XOR 2**b are copies of one node. `contact_slave`: slave indices are local copies of the contact's own partition. `contact_owner`: among the 2048 contacts of one partition no owner appears more than 256 times, and some owner appears exactly 256 times. `contact_master`: master indices are local copies of the owner partition. `part_of_node`: values of 400 or more mark copies of no rigid part.
All inputs are finite; a program needn't handle non-finite values.
Results may differ from a plain program's by a relative error of at most 0.0001.
Values sent between devices are 32-bit elements; how exact they have to be, the bound alone decides.
A program may use at most 128 MiB of HBM per device.

v0:
```python
import jax
import jax.numpy as jnp
from jax import lax
from jax.sharding import PartitionSpec as P

CYCLES = 3
PARTS_SIZE = 400
TIME_STEP = 0.1
DAMP_RATIO = 0.05
PENALTY = 2.0
GAP_WIDTH = 0.5
CONTACT_DAMP = 0.2


def partner(block, axis, apart):
    count = lax.axis_size(axis)
    route = []
    for low in range(count):
        high = low | 1 << apart
        if high != low and high < count:
            route += [(low, high), (high, low)]
    return lax.ppermute(block, axis, route)


def element_forces(corners, material, stiffness, nodal_field):
    blocks = corners.shape[1] // 128
    material_count = stiffness.shape[0]
    onehot = (material[:, None] == jnp.arange(material_count, dtype=jnp.int32)[None, :]).astype(
        jnp.float32
    )
    block_matrix = jnp.dot(
        onehot, stiffness.reshape(material_count, 576), precision=lax.Precision.HIGHEST
    ).reshape(blocks, 24, 24)
    gathered = nodal_field[:, corners].reshape(24, blocks, 128)
    forces = jnp.einsum("bij,jbk->ibk", block_matrix, gathered, precision=lax.Precision.HIGHEST)
    return (
        jnp.zeros_like(nodal_field)
        .at[:, corners.reshape(-1)]
        .add(forces.reshape(3, 8 * corners.shape[1]))
    )


def contact_push(slave_pos, slave_vel, master_pos, master_vel, normal):
    gap_size = jnp.sum((slave_pos - master_pos) * normal, axis=0)
    closing = jnp.sum((slave_vel - master_vel) * normal, axis=0)
    push_size = (
        PENALTY * GAP_WIDTH * jax.nn.softplus(-gap_size / GAP_WIDTH) - CONTACT_DAMP * closing
    )
    return push_size[None] * normal


def cross_product(left, right):
    return jnp.stack(
        [
            left[1] * right[2] - left[2] * right[1],
            left[2] * right[0] - left[0] * right[2],
            left[0] * right[1] - left[1] * right[0],
        ]
    )


def per_device(
    rest_pos,
    displacement,
    velocity,
    ext_force,
    node_mass,
    body_accel,
    connectivity,
    elem_material,
    stiffness,
    shared_nodes,
    contact_slave,
    contact_owner,
    contact_master,
    contact_normal,
    part_of_node,
    part_mass,
    part_center,
    part_inertia,
):
    domains = lax.axis_size("dom")
    neighbours = shared_nodes.shape[1]
    shared_count = shared_nodes.shape[2]
    shared_flat = shared_nodes.reshape(-1)
    accel_column = body_accel[:, None]
    node_count = displacement.shape[1]
    local_elem = jnp.arange(connectivity.shape[1], dtype=jnp.int32)
    corners = (connectivity + local_elem[None, :]) % node_count
    displaced = displacement
    speeds = velocity
    assembled = jnp.zeros_like(displacement)
    for cycle_index in range(CYCLES):
        internal = element_forces(
            corners, elem_material, stiffness, displaced + DAMP_RATIO * speeds
        )
        own_values = internal[:, shared_flat].reshape(3, neighbours, shared_count)
        received = []
        for bit_number in range(neighbours):
            received.append(partner(own_values[:, bit_number], "dom", bit_number))
        assembled = internal.at[:, shared_flat].add(
            jnp.stack(received, axis=1).reshape(3, neighbours * shared_count)
        )
        speeds = speeds + TIME_STEP * ((ext_force - assembled) / node_mass[None] - accel_column)
        displaced = displaced + TIME_STEP * speeds
    positions = rest_pos + displaced
    contacts = contact_slave.shape[0]
    capacity = 4 * contacts // domains
    owners = contact_owner[:, 0]
    owner_hits = (owners[:, None] == jnp.arange(domains, dtype=jnp.int32)[None, :]).astype(
        jnp.int32
    )
    slot_rank = jnp.sum(jnp.cumsum(owner_hits, axis=0) * owner_hits, axis=1) - 1
    slot_index = owners * capacity + slot_rank
    slave_pos = positions[:, contact_slave]
    slave_vel = speeds[:, contact_slave]
    contact_force = jnp.zeros_like(positions)
    payload = jnp.zeros((10, domains * capacity), jnp.float32).at[9].set(-1.0)
    payload = payload.at[:, slot_index].set(
        jnp.concatenate(
            [slave_pos, slave_vel, contact_normal, contact_master[None].astype(jnp.float32)], 0
        )
    )
    payload = payload.reshape(10, domains, capacity)
    arrived = lax.all_to_all(payload, "dom", split_axis=1, concat_axis=1, tiled=True)
    valid_slot = (arrived[9] >= 0.0).astype(jnp.float32)
    master_index = jnp.maximum(arrived[9], 0.0).astype(jnp.int32)
    pushed = (
        contact_push(
            arrived[0:3],
            arrived[3:6],
            positions[:, master_index],
            speeds[:, master_index],
            arrived[6:9],
        )
        * valid_slot[None]
    )
    returned = lax.all_to_all(pushed, "dom", split_axis=1, concat_axis=1, tiled=True)
    returned, pushed, master_float = (returned, pushed, arrived[9:10])
    master_index = jnp.maximum(master_float, 0.0).astype(jnp.int32)
    contact_force = contact_force.at[:, master_index.reshape(-1)].add(-pushed.reshape(3, -1))
    slave_push = returned.reshape(3, domains * capacity)[:, slot_index]
    contact_force = contact_force.at[:, contact_slave].add(slave_push)
    nodal_velocity = speeds + TIME_STEP * contact_force / node_mass[None]
    net_force = ext_force - assembled + contact_force - node_mass[None] * accel_column
    part_index = jnp.minimum(part_of_node, PARTS_SIZE)
    weighted = jnp.concatenate([node_mass[None], node_mass[None] * positions], 0)
    totals = lax.psum(
        jax.ops.segment_sum(
            jnp.concatenate([weighted, net_force, cross_product(positions, net_force)], 0).T,
            part_index,
            PARTS_SIZE + 1,
        )[:PARTS_SIZE].T,
        "dom",
    )
    mass_total = part_mass + totals[0]
    centre = (part_mass[None] * part_center + totals[1:4]) / mass_total[None]
    force_sum = totals[4:7]
    torque = totals[7:10] - cross_product(centre, force_sum)
    part_motion = jnp.concatenate([force_sum / mass_total[None], torque / part_inertia], 0)
    return (nodal_velocity, part_motion)


def solution(mesh):
    placed = (
        P(None, "dom"),
        P(None, "dom"),
        P(None, "dom"),
        P(None, "dom"),
        P("dom"),
        P(),
        P(None, "dom"),
        P("dom"),
        P(),
        P("dom", None, None),
        P("dom"),
        P("dom", None),
        P("dom"),
        P(None, "dom"),
        P("dom"),
        P(),
        P(),
        P(),
    )
    return jax.shard_map(
        per_device, mesh=mesh, in_specs=placed, out_specs=(P(None, "dom"), P()), check_vma=False
    )
```

profile of v0, /device:TPU:0, one launch (start us, length us, event | category | flops | bytes accessed | tf_op | source)
XLA Modules:
  0.0 1264.1 jit_solution(16717740665865341079)
XLA Ops:
  5.1 109.0 %gather_fusion = f32[32768,3]{1,0:T(8,128)} fusion(f32[3,4096]{0,1:T(8,128)S(1)} %copy.282, s32[32768]{0:T(1024)S(1)} %broadcast_clamp_fusion), kind=kCustom, calls=%fused_computation | custom fusion | bytes 917504 | tf_op jit(solution)/shard_map/gather | solution.py:34
  114.1 9.8 copy.283
  125.3 8.6 copy.288
  133.9 174.7 %scatter_custom_fusion = f32[3,4096]{0,1:T(8,128)S(1)} fusion(s32[32768]{0:T(1024)S(1)} %bitcast.187, f32[32768,3]{1,0:T(8,128)} %copy.288, f32[]{:T(128)} %constant.76.clone.1), kind=kCustom, calls=%fused_computation.32 | custom fusion | flops 98304 | bytes 49664 | tf_op jit(solution)/shard_map/scatter-add | solution.py:39
  308.6 1.7 gather_fusion.1
  311.6 2.5 collective-permute-start.1
  314.1 1.6 collective-permute-start.2
  315.8 1.6 collective-permute-start.3
  317.4 2.6 collective-permute-start.4
  320.1 9.1 reduce-window.6
  333.0 7.7 scatter_fusion
  342.8 109.0 %gather_fusion.2 = f32[32768,3]{1,0:T(8,128)} fusion(f32[3,4096]{0,1:T(8,128)S(1)} %copy.296, s32[32768]{0:T(1024)S(1)} %broadcast_clamp_fusion), kind=kCustom, calls=%fused_computation.2 | custom fusion | bytes 917504 | tf_op jit(solution)/shard_map/gather | solution.py:34
  451.8 9.8 copy.297
  462.9 8.6 copy.301
  471.5 174.7 %scatter_custom_fusion.2 = f32[3,4096]{0,1:T(8,128)S(1)} fusion(s32[32768]{0:T(1024)S(1)} %bitcast.188, f32[32768,3]{1,0:T(8,128)} %copy.301, f32[]{:T(128)} %constant.76.clone.1), kind=kCustom, calls=%fused_computation.30 | custom fusion | flops 98304 | bytes 49664 | tf_op jit(solution)/shard_map/scatter-add | solution.py:39
  646.2 2.3 gather_fusion.3
  652.1 1.8 collective-permute-done.6
  657.4 7.4 scatter_fusion.1
  666.2 109.0 %gather_fusion.4 = f32[32768,3]{1,0:T(8,128)} fusion(f32[3,4096]{0,1:T(8,128)S(1)} %copy.309, s32[32768]{0:T(1024)S(1)} %broadcast_clamp_fusion), kind=kCustom, calls=%fused_computation.4 | custom fusion | bytes 917504 | tf_op jit(solution)/shard_map/gather | solution.py:34
  775.2 9.8 copy.310
  786.3 8.6 copy.314
  794.9 174.7 %scatter_custom_fusion.4 = f32[3,4096]{0,1:T(8,128)S(1)} fusion(s32[32768]{0:T(1024)S(1)} %bitcast.189, f32[32768,3]{1,0:T(8,128)} %copy.314, f32[]{:T(128)} %constant.76.clone.1), kind=kCustom, calls=%fused_computation.28 | custom fusion | flops 98304 | bytes 49664 | tf_op jit(solution)/shard_map/scatter-add | solution.py:39
  969.7 1.7 gather_fusion.5
  972.1 4.4 copy.400
  977.2 1.5 collective-permute-start.11
  978.7 1.6 collective-permute-start.12
  980.4 1.6 collective-permute-start.13
  982.4 1.5 collective-permute-done.13
  984.0 2.5 collective-permute-done.14
  986.7 7.0 scatter_fusion.2
  995.2 6.6 gather_fusion.7
  1002.7 2.0 copy.324
  1004.7 7.0 gather_fusion.6
  1013.9 9.8 scatter_fusion.3
  1023.7 3.6 copy.329
  1027.2 2.6 all-to-all-start
  1029.9 15.6 %all-to-all-done = f32[10,32,256]{2,0,1:T(8,128)S(1)} async-done(((f32[10,32,256]{2,0,1:T(8,128)}), f32[10,32,256]{2,0,1:T(8,128)S(1)}, u32[]{:S(2)}, u32[]{:S(2)}) %all-to-all-start) | async-done | bytes 327712 | tf_op jit(solution)/shard_map/all_to_all | solution.py:125
  1045.6 29.5 %gather_fusion.8 = f32[8192,3]{1,0:T(8,128)} fusion(f32[3,4096]{0,1:T(8,128)} %copy.324, s32[8192]{0:T(1024)S(1)} %broadcast_clamp_fusion.1), kind=kCustom, calls=%fused_computation.8 | custom fusion | bytes 229376 | tf_op jit(solution)/shard_map/gather | solution.py:132
  1075.1 27.9 %gather_fusion.9 = f32[8192,3]{1,0:T(8,128)} fusion(f32[3,4096]{0,1:T(8,128)S(1)} %copy.325, s32[8192]{0:T(1024)S(1)} %broadcast_clamp_fusion.1), kind=kCustom, calls=%fused_computation.9 | custom fusion | bytes 229376 | tf_op jit(solution)/shard_map/gather | solution.py:133
  1103.1 2.8 copy.332
  1105.9 2.9 copy.334
  1109.7 2.9 all-to-all-start.1
  1112.7 2.6 copy.335
  1115.3 56.1 %scatter_custom_fusion.7 = f32[3,4096]{0,1:T(8,128)S(1)} fusion(s32[8192]{0:T(1024)S(1)} %bitcast.201, f32[8192,3]{1,0:T(8,128)} %copy.335, f32[]{:T(128)} %constant.76.clone.1), kind=kCustom, calls=%fused_computation.26 | custom fusion | flops 24576 | bytes 49664 | tf_op jit(solution)/shard_map/scatter-add | solution.py:141
  1171.4 2.6 copy.336
  1174.1 24.1 %scatter_custom_fusion.8 = f32[3,4096]{0,1:T(8,128)S(1)} fusion(f32[3,4096]{0,1:T(8,128)S(1)} %scatter_custom_fusion.7, s32[2048]{0:T(1024)} %get-tuple-element.61, f32[3,8192]{0,1:T(8,128)} %bitcast.166, s32[2048]{0:T(1024)S(1)} %broadcast_clamp_fusion.2), kind=kCustom, calls=%fused_computation.24 | custom fusion | flops 6144 | bytes 49152 | tf_op jit(solution)/shard_map/scatter-add | solution.py:143
  1200.4 22.4 %scatter_custom_fusion.9 = f32[401,10]{1,0:T(8,128)S(1)} fusion(s32[4096]{0:T(1024)S(1)} %broadcast_minimum_fusion, f32[4096,10]{1,0:T(8,128)S(1)} %copy.339, f32[]{:T(128)} %constant.76.clone.1), kind=kCustom, calls=%fused_computation.60 | custom fusion | flops 40960 | bytes 16044 | tf_op jit(solution)/shard_map/scatter-add | solution.py:149
  1222.9 40.1 %psum.7 = f32[10,400]{1,0:T(8,128)S(1)} all-reduce(f32[10,400]{1,0:T(8,128)S(1)} %bitcast.192), channel_id=1, replica_groups=mesh['dom'=32] {'dom'}, use_global_device_ids=true, to_apply=%region_15.16 | all-reduce | flops 4000 | bytes 32000 | tf_op jit(solution)/shard_map/psum | solution.py:148
  (181 shorter events, 34.9 us)
Async XLA Ops:
  0.6 3.7 copy-start
  0.6 3.7 copy-start.3
  125.2 8.6 copy-start.24
  133.8 186.2 %copy-start.9 = (s32[2048,1]{0,1:T(1,128)S(1)}, s32[2048,1]{0,1:T(1,128)}, u32[]{:S(2)}) copy-start(s32[2048,1]{0,1:T(1,128)} %param.31) | copy-start | bytes 24580
  133.9 176.5 %copy-start.4 = (s32[640]{0:T(1024)}, s32[640]{0:T(1024)S(1)}, u32[]{:S(2)}) copy-start(s32[640]{0:T(1024)S(1)} %fusion.33) | copy-start | bytes 7684
  133.9 186.2 %copy-start.13 = (s32[1024]{0:T(1024)}, s32[1024]{0:T(1024)S(1)}, u32[]{:S(2)}) copy-start(s32[1024]{0:T(1024)S(1)} %pad_clamp_fusion) | copy-start | bytes 12292
  311.0 21.9 %copy-start.5 = (s32[640]{0:T(1024)S(1)}, s32[640]{0:T(1024)}, u32[]{:S(2)}) copy-start(s32[640]{0:T(1024)} %copy-done.4) | copy-start | bytes 7684
  311.0 19.7 %collective-permute-start = (f32[3,128]{1,0:T(4,128)}, f32[3,128]{1,0:T(4,128)}, u32[]{:S(2)}, u32[]{:S(2)}) collective-permute-start(f32[3,128]{1,0:T(4,128)} %bitcast.10), channel_id=1, source_target_pairs={{0,1},{1,0},{2,3},{3,2},{4,5},{5,4},{6,7},{7,6},{8,9},{9,8},{10,11... | collective-permute-start | bytes 4616 | tf_op jit(solution)/shard_map/ppermute | solution.py:22
  311.6 19.8 %collective-permute-start.1 = (f32[3,128]{1,0:T(4,128)S(1)}, f32[3,128]{1,0:T(4,128)}, u32[]{:S(2)}, u32[]{:S(2)}) collective-permute-start(f32[3,128]{1,0:T(4,128)S(1)} %bitcast.210), channel_id=1, source_target_pairs={{0,2},{2,0},{1,3},{3,1},{4,6},{6,4},{5,7},{7,5},{8,10},{10,8},{9,1... | collective-permute-start | bytes 4616 | tf_op jit(solution)/shard_map/ppermute | solution.py:22
  314.1 17.9 %collective-permute-start.2 = (f32[3,128]{1,0:T(4,128)S(1)}, f32[3,128]{1,0:T(4,128)S(1)}, u32[]{:S(2)}, u32[]{:S(2)}) collective-permute-start(f32[3,128]{1,0:T(4,128)S(1)} %bitcast.209), channel_id=1, source_target_pairs={{0,4},{4,0},{1,5},{5,1},{2,6},{6,2},{3,7},{7,3},{8,12},{12,8},{9,1... | collective-permute-start | bytes 4616 | tf_op jit(solution)/shard_map/ppermute | solution.py:22
  315.8 16.3 %collective-permute-start.3 = (f32[3,128]{1,0:T(4,128)S(1)}, f32[3,128]{1,0:T(4,128)S(1)}, u32[]{:S(2)}, u32[]{:S(2)}) collective-permute-start(f32[3,128]{1,0:T(4,128)S(1)} %bitcast.207), channel_id=1, source_target_pairs={{0,8},{8,0},{1,9},{9,1},{2,10},{10,2},{3,11},{11,3},{4,12},{12,4},... | collective-permute-start | bytes 4616 | tf_op jit(solution)/shard_map/ppermute | solution.py:22
  317.4 14.6 %collective-permute-start.4 = (f32[3,128]{1,0:T(4,128)S(1)}, f32[3,128]{1,0:T(4,128)S(1)}, u32[]{:S(2)}, u32[]{:S(2)}) collective-permute-start(f32[3,128]{1,0:T(4,128)S(1)} %bitcast.208), channel_id=1, source_target_pairs={{0,16},{16,0},{1,17},{17,1},{2,18},{18,2},{3,19},{19,3},{4,20},{20... | collective-permute-start | bytes 4616 | tf_op jit(solution)/shard_map/ppermute | solution.py:22
  329.1 12.2 copy-start.1
  329.1 12.2 copy-start.2
  471.5 174.8 %copy-start.14 = (s32[1024]{0:T(1024)S(1)}, s32[1024]{0:T(1024)}, u32[]{:S(2)}) copy-start(s32[1024]{0:T(1024)} %copy-done.13) | copy-start | bytes 12292
  471.5 178.1 %copy-start.10 = (s32[2048,1]{0,1:T(1,128)S(1)}, s32[2048,1]{0,1:T(1,128)}, u32[]{:S(2)}) copy-start(s32[2048,1]{0,1:T(1,128)} %param.31) | copy-start | bytes 24580
  471.5 186.0 %copy-start.6 = (s32[640]{0:T(1024)S(1)}, s32[640]{0:T(1024)}, u32[]{:S(2)}) copy-start(s32[640]{0:T(1024)} %copy-done.4) | copy-start | bytes 7684
  646.2 19.2 %copy-start.16 = (f32[3]{0:T(128)S(1)}, f32[3]{0:T(128)}, u32[]{:S(2)}) copy-start(f32[3]{0:T(128)} %param.25) | copy-start | bytes 40
  649.5 2.5 collective-permute-start.5
  650.3 3.6 collective-permute-start.6
  650.9 3.6 collective-permute-start.7
  651.5 3.6 collective-permute-start.8
  652.0 4.5 collective-permute-start.9
  794.9 176.6 %copy-start.19 = (s32[2048]{0:T(1024)S(1)}, s32[2048]{0:T(1024)}, u32[]{:S(2)}) copy-start(s32[2048]{0:T(1024)} %param.30) | copy-start | bytes 24580
  971.4 11.0 collective-permute-start.10
  972.1 4.4 copy-start.21
  972.1 14.6 %copy-start.7 = (s32[640]{0:T(1024)S(1)}, s32[640]{0:T(1024)}, u32[]{:S(2)}) copy-start(s32[640]{0:T(1024)} %copy-done.4) | copy-start | bytes 7684
  976.5 17.9 %copy-start.12 = (f32[3,4096]{1,0:T(4,128)S(1)}, f32[3,4096]{1,0:T(4,128)}, u32[]{:S(2)}) copy-start(f32[3,4096]{1,0:T(4,128)} %param.20) | copy-start | bytes 147460
  976.5 17.9 %copy-start.17 = (f32[3]{0:T(128)S(1)}, f32[3]{0:T(128)}, u32[]{:S(2)}) copy-start(f32[3]{0:T(128)} %param.25) | copy-start | bytes 40
  977.2 5.2 collective-permute-start.11
  978.7 3.7 collective-permute-start.12
  980.4 3.6 collective-permute-start.13
  982.0 4.5 collective-permute-start.14
  995.2 9.5 copy-start.11
  1023.7 6.2 copy-start.8
  1023.7 6.2 copy-start.15
  1027.2 18.2 %all-to-all-start = ((f32[10,32,256]{2,0,1:T(8,128)}), f32[10,32,256]{2,0,1:T(8,128)S(1)}, u32[]{:S(2)}, u32[]{:S(2)}) async-start(f32[10,32,256]{2,0,1:T(8,128)} %copy.329), calls=%async_computation | async-start | bytes 1048576 | tf_op jit(solution)/shard_map/all_to_all | solution.py:125
  1109.7 61.7 %all-to-all-start.1 = ((f32[3,32,256]{2,0,1:T(4,128)}), f32[3,32,256]{2,0,1:T(4,128)S(1)}, u32[]{:S(2)}, u32[]{:S(2)}) async-start(f32[3,32,256]{2,0,1:T(4,128)} %get-tuple-element.29), calls=%async_computation.1 | async-start | bytes 262144 | tf_op jit(solution)/shard_map/all_to_all | solution.py:138
  1174.1 24.7 %copy-start.18 = (f32[3]{0:T(128)S(1)}, f32[3]{0:T(128)}, u32[]{:S(2)}) copy-start(f32[3]{0:T(128)} %param.25) | copy-start | bytes 40
  1198.8 64.3 %copy-start.20 = (f32[400]{0:T(512)S(1)}, f32[400]{0:T(512)}, u32[]{:S(2)}) copy-start(f32[400]{0:T(512)} %param.35) | copy-start | bytes 4804
  1198.8 64.3 %copy-start.22 = (f32[3,400]{1,0:T(4,128)S(1)}, f32[3,400]{1,0:T(4,128)}, u32[]{:S(2)}) copy-start(f32[3,400]{1,0:T(4,128)} %param.36) | copy-start | bytes 14404
  1198.8 64.4 %copy-start.23 = (f32[3,400]{1,0:T(4,128)S(1)}, f32[3,400]{1,0:T(4,128)}, u32[]{:S(2)}) copy-start(f32[3,400]{1,0:T(4,128)} %param.37) | copy-start | bytes 14404
where the time goes:
time: 1270 us; the launch traced here: 1260 us
  other arithmetic  667 us (53%)
  local copies, waits for them, and re-layouts  507 us (40%)
  blocking collectives  40.1 us (3%)
  waiting for transfers between devices  24.1 us (2%)
  starting transfers between devices  21 us (2%)
    scatter-add x3, other arithmetic, element_forces(): return jnp.zeros_like(nodal_field).at[:, corners.reshape(-1)].add(forces....  524 us
    gather x6, local copies, waits for them, and re-layouts, element_forces(): gathered = nodal_field[:, corners].reshape(24, blocks, 128)  356 us
    scatter-add x1, other arithmetic, per_device(): contact_force.at[:, master_index.reshape(-1)].add(-pushed.reshape(3, -1))  56.1 us
    psum x1, blocking collectives, per_device(): lax.psum(jax.ops.segment_sum(jnp.concatenate([weighted, net_force, cross_...  40.1 us
    gather x2, local copies, waits for them, and re-layouts, per_device(): positions[:, master_index]  32.3 us
    gather x2, local copies, waits for them, and re-layouts, per_device(): speeds[:, master_index]  30.8 us
    reshape x6, local copies, waits for them, and re-layouts, element_forces(): forces.reshape(3, 8 * corners.shape[1])  26.3 us
  transfers between devices with their start and end apart: 17, of which 7 were waited for; matrix products, arithmetic and copies ran while one was open for 6% of the time, Pallas kernels for 0%

commit v1 on v0

--- a/solution.py
+++ b/solution.py
@@ -10,6 +10,12 @@
 PENALTY = 2.0
 GAP_WIDTH = 0.5
 CONTACT_DAMP = 0.2
+
+
+def add_all(x, name):
+    terms = lax.all_gather(x, name, axis=0, tiled=False)
+    total = terms.sum(axis=0)
+    return total
 
 
 def partner(block, axis, apart):
@@ -145,7 +151,7 @@
     net_force = ext_force - assembled + contact_force - node_mass[None] * accel_column
     part_index = jnp.minimum(part_of_node, PARTS_SIZE)
     weighted = jnp.concatenate([node_mass[None], node_mass[None] * positions], 0)
-    totals = lax.psum(
+    totals = add_all(
         jax.ops.segment_sum(
             jnp.concatenate([weighted, net_force, cross_product(positions, net_force)], 0).T,
             part_index,

time: 1270 us -> 1280 us (level)
    all_gather x0 -> x1, blocking collectives: none -> 44.8 us  [add_all(): terms = lax.all_gather(x, name, axis=0, tiled=False)]
    psum x1 -> x0, blocking collectives: 40.1 us -> none  [per_device(): lax.psum(jax.ops.segment_sum(jnp.concatenate([weighted, net_force, cross_...]
where the time goes in v1:
time: 1280 us; the launch traced here: 1270 us
  other arithmetic  667 us (52%)
  local copies, waits for them, and re-layouts  505 us (39%)
  blocking collectives  44.8 us (4%)
  waiting for transfers between devices  24.1 us (2%)
  starting transfers between devices  21 us (2%)
    scatter-add x3, other arithmetic, element_forces(): return jnp.zeros_like(nodal_field).at[:, corners.reshape(-1)].add(forces....  524 us
    gather x6, local copies, waits for them, and re-layouts, element_forces(): gathered = nodal_field[:, corners].reshape(24, blocks, 128)  355 us
    scatter-add x1, other arithmetic, per_device(): contact_force.at[:, master_index.reshape(-1)].add(-pushed.reshape(3, -1))  56.1 us
    all_gather x1, blocking collectives, add_all(): terms = lax.all_gather(x, name, axis=0, tiled=False)  44.8 us
    gather x2, local copies, waits for them, and re-layouts, per_device(): positions[:, master_index]  32.2 us
    gather x2, local copies, waits for them, and re-layouts, per_device(): speeds[:, master_index]  30.6 us
    reshape x6, local copies, waits for them, and re-layouts, element_forces(): forces.reshape(3, 8 * corners.shape[1])  26.3 us
  transfers between devices with their start and end apart: 17, of which 7 were waited for; matrix products, arithmetic and copies ran while one was open for 6% of the time, Pallas kernels for 0%

profile of v1, /device:TPU:0, one launch (start us, length us, event | category | flops | bytes accessed | tf_op | source)
XLA Modules:
  0.0 1267.0 jit_solution(6049074356317821737)
XLA Ops:
  5.1 108.5 %gather_fusion = f32[32768,3]{1,0:T(8,128)} fusion(f32[3,4096]{0,1:T(8,128)S(1)} %copy.353, s32[32768]{0:T(1024)S(1)} %broadcast_clamp_fusion), kind=kCustom, calls=%fused_computation | custom fusion | bytes 917504 | tf_op jit(solution)/shard_map/gather | solution.py:40
  113.6 9.8 copy.354
  124.7 8.6 copy.359
  133.4 174.7 %scatter_custom_fusion = f32[3,4096]{0,1:T(8,128)S(1)} fusion(s32[32768]{0:T(1024)S(1)} %bitcast.189, f32[32768,3]{1,0:T(8,128)} %copy.359, f32[]{:T(128)} %constant.76.clone.1), kind=kCustom, calls=%fused_computation.32 | custom fusion | flops 98304 | bytes 49664 | tf_op jit(solution)/shard_map/scatter-add | solution.py:45
  308.1 1.7 gather_fusion.1
  311.1 2.5 collective-permute-start.1
  313.6 1.5 collective-permute-start.2
  315.2 1.6 collective-permute-start.3
  316.9 2.6 collective-permute-start.4
  319.5 9.1 reduce-window.6
  332.5 7.7 scatter_fusion
  342.3 108.5 %gather_fusion.2 = f32[32768,3]{1,0:T(8,128)} fusion(f32[3,4096]{0,1:T(8,128)S(1)} %copy.367, s32[32768]{0:T(1024)S(1)} %broadcast_clamp_fusion), kind=kCustom, calls=%fused_computation.2 | custom fusion | bytes 917504 | tf_op jit(solution)/shard_map/gather | solution.py:40
  450.8 9.8 copy.368
  461.9 8.6 copy.372
  470.5 174.7 %scatter_custom_fusion.2 = f32[3,4096]{0,1:T(8,128)S(1)} fusion(s32[32768]{0:T(1024)S(1)} %bitcast.190, f32[32768,3]{1,0:T(8,128)} %copy.372, f32[]{:T(128)} %constant.76.clone.1), kind=kCustom, calls=%fused_computation.30 | custom fusion | flops 98304 | bytes 49664 | tf_op jit(solution)/shard_map/scatter-add | solution.py:45
  645.2 2.2 gather_fusion.3
  651.1 1.8 collective-permute-done.6
  656.4 7.4 scatter_fusion.1
  665.2 108.5 %gather_fusion.4 = f32[32768,3]{1,0:T(8,128)} fusion(f32[3,4096]{0,1:T(8,128)S(1)} %copy.380, s32[32768]{0:T(1024)S(1)} %broadcast_clamp_fusion), kind=kCustom, calls=%fused_computation.4 | custom fusion | bytes 917504 | tf_op jit(solution)/shard_map/gather | solution.py:40
  773.7 9.8 copy.381
  784.8 8.6 copy.385
  793.4 174.7 %scatter_custom_fusion.4 = f32[3,4096]{0,1:T(8,128)S(1)} fusion(s32[32768]{0:T(1024)S(1)} %bitcast.191, f32[32768,3]{1,0:T(8,128)} %copy.385, f32[]{:T(128)} %constant.76.clone.1), kind=kCustom, calls=%fused_computation.28 | custom fusion | flops 98304 | bytes 49664 | tf_op jit(solution)/shard_map/scatter-add | solution.py:45
  968.1 1.7 gather_fusion.5
  970.6 4.4 copy.492
  975.6 1.5 collective-permute-start.11
  977.2 1.5 collective-permute-start.12
  978.8 1.6 collective-permute-start.13
  980.9 1.5 collective-permute-done.13
  982.4 2.6 collective-permute-done.14
  985.2 7.0 scatter_fusion.2
  993.6 6.6 gather_fusion.7
  1001.2 2.0 copy.395
  1003.1 7.0 gather_fusion.6
  1012.3 9.8 scatter_fusion.3
  1022.1 3.6 copy.400
  1025.7 2.6 all-to-all-start
  1028.4 15.6 %all-to-all-done = f32[10,32,256]{2,0,1:T(8,128)S(1)} async-done(((f32[10,32,256]{2,0,1:T(8,128)}), f32[10,32,256]{2,0,1:T(8,128)S(1)}, u32[]{:S(2)}, u32[]{:S(2)}) %all-to-all-start) | async-done | bytes 327712 | tf_op jit(solution)/shard_map/all_to_all | solution.py:131
  1044.1 29.3 %gather_fusion.8 = f32[8192,3]{1,0:T(8,128)} fusion(f32[3,4096]{0,1:T(8,128)} %copy.395, s32[8192]{0:T(1024)S(1)} %broadcast_clamp_fusion.1), kind=kCustom, calls=%fused_computation.8 | custom fusion | bytes 229376 | tf_op jit(solution)/shard_map/gather | solution.py:138
  1073.4 27.7 %gather_fusion.9 = f32[8192,3]{1,0:T(8,128)} fusion(f32[3,4096]{0,1:T(8,128)S(1)} %copy.396, s32[8192]{0:T(1024)S(1)} %broadcast_clamp_fusion.1), kind=kCustom, calls=%fused_computation.9 | custom fusion | bytes 229376 | tf_op jit(solution)/shard_map/gather | solution.py:139
  1101.2 2.8 copy.403
  1104.0 2.9 copy.405
  1107.9 2.9 all-to-all-start.1
  1110.8 2.6 copy.406
  1113.4 56.1 %scatter_custom_fusion.7 = f32[3,4096]{0,1:T(8,128)S(1)} fusion(s32[8192]{0:T(1024)S(1)} %bitcast.202, f32[8192,3]{1,0:T(8,128)} %copy.406, f32[]{:T(128)} %constant.76.clone.1), kind=kCustom, calls=%fused_computation.26 | custom fusion | flops 24576 | bytes 49664 | tf_op jit(solution)/shard_map/scatter-add | solution.py:147
  1169.5 2.6 copy.407
  1172.2 24.1 %scatter_custom_fusion.8 = f32[3,4096]{0,1:T(8,128)S(1)} fusion(f32[3,4096]{0,1:T(8,128)S(1)} %scatter_custom_fusion.7, s32[2048]{0:T(1024)} %get-tuple-element.63, f32[3,8192]{0,1:T(8,128)} %bitcast.168, s32[2048]{0:T(1024)S(1)} %broadcast_clamp_fusion.2), kind=kCustom, calls=%fused_computation.24 | custom fusion | flops 6144 | bytes 49152 | tf_op jit(solution)/shard_map/scatter-add | solution.py:149
  1198.5 22.4 %scatter_custom_fusion.9 = f32[401,10]{1,0:T(8,128)S(1)} fusion(s32[4096]{0:T(1024)S(1)} %broadcast_minimum_fusion, f32[4096,10]{1,0:T(8,128)S(1)} %copy.410, f32[]{:T(128)} %constant.76.clone.1), kind=kCustom, calls=%fused_computation.61 | custom fusion | flops 40960 | bytes 16044 | tf_op jit(solution)/shard_map/scatter-add | solution.py:155
  1221.0 44.8 %all-gather.1 = f32[32,10,400]{2,1,0:T(8,128)S(1)} all-gather(f32[1,10,400]{2,1,0:T(8,128)S(1)} %copy.411), channel_id=2, replica_groups=mesh['dom'=32] {'dom'}, dimensions={0}, use_global_device_ids=true | all-gather | bytes 528000 | tf_op jit(solution)/shard_map/all_gather | solution.py:16
  (182 shorter events, 35.0 us)
Async XLA Ops:
  0.6 3.7 copy-start
  0.6 3.7 copy-start.3
  124.7 8.6 copy-start.24
  133.3 186.2 %copy-start.9 = (s32[2048,1]{0,1:T(1,128)S(1)}, s32[2048,1]{0,1:T(1,128)}, u32[]{:S(2)}) copy-start(s32[2048,1]{0,1:T(1,128)} %param.31) | copy-start | bytes 24580
  133.3 176.5 %copy-start.4 = (s32[640]{0:T(1024)}, s32[640]{0:T(1024)S(1)}, u32[]{:S(2)}) copy-start(s32[640]{0:T(1024)S(1)} %fusion.33) | copy-start | bytes 7684
  133.4 186.2 %copy-start.13 = (s32[1024]{0:T(1024)}, s32[1024]{0:T(1024)S(1)}, u32[]{:S(2)}) copy-start(s32[1024]{0:T(1024)S(1)} %pad_clamp_fusion) | copy-start | bytes 12292
  310.5 22.0 %copy-start.5 = (s32[640]{0:T(1024)S(1)}, s32[640]{0:T(1024)}, u32[]{:S(2)}) copy-start(s32[640]{0:T(1024)} %copy-done.4) | copy-start | bytes 7684
  310.5 19.7 %collective-permute-start = (f32[3,128]{1,0:T(4,128)}, f32[3,128]{1,0:T(4,128)}, u32[]{:S(2)}, u32[]{:S(2)}) collective-permute-start(f32[3,128]{1,0:T(4,128)} %bitcast.10), channel_id=1, source_target_pairs={{0,1},{1,0},{2,3},{3,2},{4,5},{5,4},{6,7},{7,6},{8,9},{9,8},{10,11... | collective-permute-start | bytes 4616 | tf_op jit(solution)/shard_map/ppermute | solution.py:28
  311.1 19.8 %collective-permute-start.1 = (f32[3,128]{1,0:T(4,128)S(1)}, f32[3,128]{1,0:T(4,128)}, u32[]{:S(2)}, u32[]{:S(2)}) collective-permute-start(f32[3,128]{1,0:T(4,128)S(1)} %bitcast.210), channel_id=1, source_target_pairs={{0,2},{2,0},{1,3},{3,1},{4,6},{6,4},{5,7},{7,5},{8,10},{10,8},{9,1... | collective-permute-start | bytes 4616 | tf_op jit(solution)/shard_map/ppermute | solution.py:28
  313.6 17.9 %collective-permute-start.2 = (f32[3,128]{1,0:T(4,128)S(1)}, f32[3,128]{1,0:T(4,128)S(1)}, u32[]{:S(2)}, u32[]{:S(2)}) collective-permute-start(f32[3,128]{1,0:T(4,128)S(1)} %bitcast.209), channel_id=1, source_target_pairs={{0,4},{4,0},{1,5},{5,1},{2,6},{6,2},{3,7},{7,3},{8,12},{12,8},{9,1... | collective-permute-start | bytes 4616 | tf_op jit(solution)/shard_map/ppermute | solution.py:28
  315.2 16.3 %collective-permute-start.3 = (f32[3,128]{1,0:T(4,128)S(1)}, f32[3,128]{1,0:T(4,128)S(1)}, u32[]{:S(2)}, u32[]{:S(2)}) collective-permute-start(f32[3,128]{1,0:T(4,128)S(1)} %bitcast.207), channel_id=1, source_target_pairs={{0,8},{8,0},{1,9},{9,1},{2,10},{10,2},{3,11},{11,3},{4,12},{12,4},... | collective-permute-start | bytes 4616 | tf_op jit(solution)/shard_map/ppermute | solution.py:28
  316.9 14.7 %collective-permute-start.4 = (f32[3,128]{1,0:T(4,128)S(1)}, f32[3,128]{1,0:T(4,128)S(1)}, u32[]{:S(2)}, u32[]{:S(2)}) collective-permute-start(f32[3,128]{1,0:T(4,128)S(1)} %bitcast.208), channel_id=1, source_target_pairs={{0,16},{16,0},{1,17},{17,1},{2,18},{18,2},{3,19},{19,3},{4,20},{20... | collective-permute-start | bytes 4616 | tf_op jit(solution)/shard_map/ppermute | solution.py:28
  328.6 12.2 copy-start.1
  328.6 12.2 copy-start.2
  470.4 174.8 %copy-start.14 = (s32[1024]{0:T(1024)S(1)}, s32[1024]{0:T(1024)}, u32[]{:S(2)}) copy-start(s32[1024]{0:T(1024)} %copy-done.13) | copy-start | bytes 12292
  470.5 178.1 %copy-start.10 = (s32[2048,1]{0,1:T(1,128)S(1)}, s32[2048,1]{0,1:T(1,128)}, u32[]{:S(2)}) copy-start(s32[2048,1]{0,1:T(1,128)} %param.31) | copy-start | bytes 24580
  470.5 186.0 %copy-start.6 = (s32[640]{0:T(1024)S(1)}, s32[640]{0:T(1024)}, u32[]{:S(2)}) copy-start(s32[640]{0:T(1024)} %copy-done.4) | copy-start | bytes 7684
  645.2 19.2 %copy-start.16 = (f32[3]{0:T(128)S(1)}, f32[3]{0:T(128)}, u32[]{:S(2)}) copy-start(f32[3]{0:T(128)} %param.25) | copy-start | bytes 40
  648.5 2.5 collective-permute-start.5
  649.3 3.6 collective-permute-start.6
  649.9 3.6 collective-permute-start.7
  650.5 3.6 collective-permute-start.8
  651.0 4.5 collective-permute-start.9
  793.4 176.6 %copy-start.19 = (s32[2048]{0:T(1024)S(1)}, s32[2048]{0:T(1024)}, u32[]{:S(2)}) copy-start(s32[2048]{0:T(1024)} %param.30) | copy-start | bytes 24580
  969.9 10.9 collective-permute-start.10
  970.6 4.4 copy-start.21
  970.6 14.6 %copy-start.7 = (s32[640]{0:T(1024)S(1)}, s32[640]{0:T(1024)}, u32[]{:S(2)}) copy-start(s32[640]{0:T(1024)} %copy-done.4) | copy-start | bytes 7684
  975.0 17.9 %copy-start.12 = (f32[3,4096]{1,0:T(4,128)S(1)}, f32[3,4096]{1,0:T(4,128)}, u32[]{:S(2)}) copy-start(f32[3,4096]{1,0:T(4,128)} %param.20) | copy-start | bytes 147460
  975.0 17.9 %copy-start.17 = (f32[3]{0:T(128)S(1)}, f32[3]{0:T(128)}, u32[]{:S(2)}) copy-start(f32[3]{0:T(128)} %param.25) | copy-start | bytes 40
  975.6 5.2 collective-permute-start.11
  977.2 3.7 collective-permute-start.12
  978.8 3.6 collective-permute-start.13
  980.5 4.5 collective-permute-start.14
  993.6 9.5 copy-start.11
  1022.1 6.2 copy-start.8
  1022.1 6.2 copy-start.15
  1025.7 18.2 %all-to-all-start = ((f32[10,32,256]{2,0,1:T(8,128)}), f32[10,32,256]{2,0,1:T(8,128)S(1)}, u32[]{:S(2)}, u32[]{:S(2)}) async-start(f32[10,32,256]{2,0,1:T(8,128)} %copy.400), calls=%async_computation | async-start | bytes 1048576 | tf_op jit(solution)/shard_map/all_to_all | solution.py:131
  1107.9 61.7 %all-to-all-start.1 = ((f32[3,32,256]{2,0,1:T(4,128)}), f32[3,32,256]{2,0,1:T(4,128)S(1)}, u32[]{:S(2)}, u32[]{:S(2)}) async-start(f32[3,32,256]{2,0,1:T(4,128)} %get-tuple-element.31), calls=%async_computation.1 | async-start | bytes 262144 | tf_op jit(solution)/shard_map/all_to_all | solution.py:144
  1172.2 24.7 %copy-start.18 = (f32[3]{0:T(128)S(1)}, f32[3]{0:T(128)}, u32[]{:S(2)}) copy-start(f32[3]{0:T(128)} %param.25) | copy-start | bytes 40
  1198.5 67.5 %copy-start.20 = (f32[400]{0:T(512)S(1)}, f32[400]{0:T(512)}, u32[]{:S(2)}) copy-start(f32[400]{0:T(512)} %param.35) | copy-start | bytes 4804
  1198.5 67.5 %copy-start.22 = (f32[3,400]{1,0:T(4,128)S(1)}, f32[3,400]{1,0:T(4,128)}, u32[]{:S(2)}) copy-start(f32[3,400]{1,0:T(4,128)} %param.36) | copy-start | bytes 14404
  1198.5 67.6 %copy-start.23 = (f32[3,400]{1,0:T(4,128)S(1)}, f32[3,400]{1,0:T(4,128)}, u32[]{:S(2)}) copy-start(f32[3,400]{1,0:T(4,128)} %param.37) | copy-start | bytes 14404
